TPU v7x, 32 devices: a whole 2x2x4 slice. The times are simulated.
32 devices in a mesh: replica: 16 (over z, x, core), shard: 2 (over y).
Axes of the slice: x: 2, y: 2, z: 4, core: 2. Of those that a mesh axis runs over, the one named last changes fastest.
Arguments:
- tokens: bfloat16 [8192, 768], P(('replica', 'shard')), may hold values from -32 to 32
- lengths: int32 [32], P(('replica', 'shard')), may hold values from 1 to 256, 5120 in all
- cotangent: bfloat16 [8192, 768], P(('replica', 'shard')), may hold values from -6 to 6
- w_qkv: bfloat16 [768, 2304], P('shard'), may hold values from -0.14433757 to 0.14433757
- bias_q: bfloat16 [768], P('shard'), may hold values from -3 to 3
- bias_v: bfloat16 [768], P('shard'), may hold values from -3 to 3
- w_out: bfloat16 [768, 768], P('shard'), may hold values from -1.75 to 1.75
- bias_out: bfloat16 [768], P('shard'), may hold values from -3 to 3
- gain_attn: bfloat16 [768], P('shard'), may hold values from 0.5 to 1.5
- shift_attn: bfloat16 [768], P('shard'), may hold values from -3 to 3
- w_in: bfloat16 [768, 3072], P('shard'), may hold values from -0.21875 to 0.21875
- bias_in: bfloat16 [3072], P('shard'), may hold values from -3 to 3
- w_back: bfloat16 [3072, 768], P('shard'), may hold values from -0.109375 to 0.109375
- bias_back: bfloat16 [768], P('shard'), may hold values from -3 to 3
- gain_ffn: bfloat16 [768], P('shard'), may hold values from 0.5 to 1.5
- shift_ffn: bfloat16 [768], P('shard'), may hold values from -3 to 3
Outputs:
- block_out: bfloat16 [8192, 768], P(('replica', 'shard'))
- grad_tokens: float32 [8192, 768], P(('replica', 'shard'))
- grad_w_qkv: float32 [768, 2304], P('shard')
- grad_bias_q: float32 [768], P('shard')
- grad_bias_v: float32 [768], P('shard')
- grad_w_out: float32 [768, 768], P('shard')
- grad_bias_out: float32 [768], P('shard')
- grad_gain_attn: float32 [768], P('shard')
- grad_shift_attn: float32 [768], P('shard')
- grad_w_in: float32 [768, 3072], P('shard')
- grad_bias_in: float32 [3072], P('shard')
- grad_w_back: float32 [3072, 768], P('shard')
- grad_bias_back: float32 [768], P('shard')
- grad_gain_ffn: float32 [768], P('shard')
- grad_shift_ffn: float32 [768], P('shard')
Inputs may be any that keep to these rules, and one draw needn't show every extreme that they name: `lengths`: each sequence has at least one live token; the longest has exactly 256.
All inputs are finite; a program needn't handle non-finite values. No bound on the sum of `lengths` on one device may be relied on, other than what follows from the above.
Results may differ from a plain program's by a relative error of at most 0.012.
The roundings to bfloat16 on the way count: a program that leaves them out, or rounds other values in their place, can miss the bound.
Values may be sent and summed in bfloat16 or wider, within the bound.
A program may use at most 192 MiB of HBM per device.

v0:
```python
import jax
import jax.numpy as jnp
from jax import lax
from jax.sharding import PartitionSpec as P

HEADS = 12
HEAD_DIM = 64


def product(form, left, right):
    return jnp.einsum(form, left, right, preferred_element_type=jnp.float32)


def normalize(hidden):
    average = jnp.mean(hidden, axis=-1, keepdims=True)
    centred = hidden - average
    inv_std = lax.rsqrt(jnp.mean(centred * centred, axis=-1, keepdims=True) + 1e-12)
    return (centred * inv_std, inv_std)


def norm_back(grad_in, normed, inv_std, gain):
    grad_norm = grad_in * gain
    return inv_std * (
        grad_norm
        - jnp.mean(grad_norm, axis=-1, keepdims=True)
        - normed * jnp.mean(grad_norm * normed, axis=-1, keepdims=True)
    )


def gelu_slope(pre):
    return (
        0.5 * (1.0 + lax.erf(pre * 0.7071067811865476))
        + pre * jnp.exp(-0.5 * pre * pre) * 0.3989422804014327
    )


def on_device(
    tokens,
    lengths,
    cotangent,
    w_qkv,
    bias_q,
    bias_v,
    w_out,
    bias_out,
    gain_attn,
    shift_attn,
    w_in,
    bias_in,
    w_back,
    bias_back,
    gain_ffn,
    shift_ffn,
):
    bf16 = jnp.bfloat16
    f32 = jnp.float32
    full = (
        lax.all_gather(w_qkv, "shard", axis=0, tiled=True),
        lax.all_gather(bias_q, "shard", axis=0, tiled=True),
        lax.all_gather(bias_v, "shard", axis=0, tiled=True),
        lax.all_gather(w_out, "shard", axis=0, tiled=True),
        lax.all_gather(bias_out, "shard", axis=0, tiled=True),
        lax.all_gather(gain_attn, "shard", axis=0, tiled=True),
        lax.all_gather(shift_attn, "shard", axis=0, tiled=True),
        lax.all_gather(w_in, "shard", axis=0, tiled=True),
        lax.all_gather(bias_in, "shard", axis=0, tiled=True),
        lax.all_gather(w_back, "shard", axis=0, tiled=True),
        lax.all_gather(bias_back, "shard", axis=0, tiled=True),
        lax.all_gather(gain_ffn, "shard", axis=0, tiled=True),
        lax.all_gather(shift_ffn, "shard", axis=0, tiled=True),
    )
    f_qkv, f_bq, f_bv, f_out, f_bo, f_ga, f_sa, f_in, f_bi, f_back, f_bb, f_gf, f_sf = full
    group = lengths.shape[0]
    span = tokens.shape[0] // group
    width = tokens.shape[1]
    scale = HEAD_DIM ** (-0.5)
    factor = float(tokens.shape[0] * lax.axis_size("replica") * lax.axis_size("shard")) ** (-0.5)
    live = jnp.arange(span, dtype=jnp.int32)[None, :] < lengths[:, None]
    inputs = tokens.reshape(group, span, width)
    qkv = product("bld,de->ble", inputs, f_qkv)
    query = (qkv[..., :width] + f_bq.astype(f32)).astype(bf16).reshape(group, span, HEADS, HEAD_DIM)
    keys = qkv[..., width : 2 * width].astype(bf16).reshape(group, span, HEADS, HEAD_DIM)
    values = (
        (qkv[..., 2 * width :] + f_bv.astype(f32))
        .astype(bf16)
        .reshape(group, span, HEADS, HEAD_DIM)
    )

    def make_scores():
        raw = product("bqhe,bkhe->bhqk", query, keys) * scale
        return jnp.where(live[:, None, None, :], raw, -1000000000.0)

    scores = make_scores()
    top = jnp.max(scores, axis=-1, keepdims=True)
    expo = jnp.exp(scores - top)
    total = jnp.sum(expo, axis=-1, keepdims=True)
    log_total = top + jnp.log(total)
    attend = (expo / total).astype(bf16)
    context = product("bhqk,bkhe->bqhe", attend, values).reshape(group, span, width).astype(bf16)
    resid_one = inputs.astype(f32) + product("bld,de->ble", context, f_out) + f_bo.astype(f32)
    normed_one, inv_one = normalize(resid_one)
    gain_one = f_ga.astype(f32)
    mid = normed_one * gain_one + f_sa.astype(f32)
    mid_b = mid.astype(bf16)
    pre = product("bld,df->blf", mid_b, f_in) + f_bi.astype(f32)
    act = (0.5 * pre * (1.0 + lax.erf(pre * 0.7071067811865476))).astype(bf16)
    resid_two = mid + product("blf,fd->bld", act, f_back) + f_bb.astype(f32)
    normed_two, inv_two = normalize(resid_two)
    gain_two = f_gf.astype(f32)
    block_out = (normed_two * gain_two + f_sf.astype(f32)).astype(bf16)
    again = (
        lax.all_gather(w_qkv, "shard", axis=0, tiled=True),
        lax.all_gather(bias_q, "shard", axis=0, tiled=True),
        lax.all_gather(bias_v, "shard", axis=0, tiled=True),
        lax.all_gather(w_out, "shard", axis=0, tiled=True),
        lax.all_gather(bias_out, "shard", axis=0, tiled=True),
        lax.all_gather(gain_attn, "shard", axis=0, tiled=True),
        lax.all_gather(shift_attn, "shard", axis=0, tiled=True),
        lax.all_gather(w_in, "shard", axis=0, tiled=True),
        lax.all_gather(bias_in, "shard", axis=0, tiled=True),
        lax.all_gather(w_back, "shard", axis=0, tiled=True),
        lax.all_gather(bias_back, "shard", axis=0, tiled=True),
        lax.all_gather(gain_ffn, "shard", axis=0, tiled=True),
        lax.all_gather(shift_ffn, "shard", axis=0, tiled=True),
    )
    b_qkv = again[0]
    b_out = again[3]
    b_in = again[7]
    b_back = again[9]
    grad_out = cotangent.reshape(group, span, width).astype(f32) * live[..., None].astype(f32)
    g_gain_ffn = jnp.sum(grad_out * normed_two, axis=(0, 1))
    g_shift_ffn = jnp.sum(grad_out, axis=(0, 1))
    grad_two = norm_back(grad_out, normed_two, inv_two, gain_two)
    grad_two_b = grad_two.astype(bf16)
    g_w_back = product("blf,bld->fd", act, grad_two_b)
    g_bias_back = jnp.sum(grad_two, axis=(0, 1))
    grad_pre = product("bld,fd->blf", grad_two_b, b_back) * gelu_slope(pre)
    grad_pre_b = grad_pre.astype(bf16)
    g_w_in = product("bld,blf->df", mid_b, grad_pre_b)
    g_bias_in = jnp.sum(grad_pre, axis=(0, 1))
    grad_mid = grad_two + product("blf,df->bld", grad_pre_b, b_in)
    g_gain_attn = jnp.sum(grad_mid * normed_one, axis=(0, 1))
    g_shift_attn = jnp.sum(grad_mid, axis=(0, 1))
    grad_one = norm_back(grad_mid, normed_one, inv_one, gain_one)
    grad_one_b = grad_one.astype(bf16)
    g_w_out = product("bld,ble->de", context, grad_one_b)
    g_bias_out = jnp.sum(grad_one, axis=(0, 1))
    grad_ctx = (
        product("ble,de->bld", grad_one_b, b_out).astype(bf16).reshape(group, span, HEADS, HEAD_DIM)
    )
    weights_again = jnp.exp(make_scores() - log_total)
    weights_b = weights_again.astype(bf16)
    grad_att = product("bqhe,bkhe->bhqk", grad_ctx, values)
    grad_values = product("bhqk,bqhe->bkhe", weights_b, grad_ctx).reshape(group, span, width)
    delta = jnp.sum(weights_again * grad_att, axis=-1, keepdims=True)
    grad_scores = (weights_again * (grad_att - delta) * scale).astype(bf16)
    grad_query = product("bhqk,bkhe->bqhe", grad_scores, keys).reshape(group, span, width)
    grad_keys = product("bhqk,bqhe->bkhe", grad_scores, query).reshape(group, span, width)
    grad_qkv_b = jnp.concatenate([grad_query, grad_keys, grad_values], axis=-1).astype(bf16)
    g_w_qkv = product("bld,ble->de", inputs, grad_qkv_b)
    g_bias_q = jnp.sum(grad_query, axis=(0, 1))
    g_bias_v = jnp.sum(grad_values, axis=(0, 1))
    grad_input = grad_one + product("ble,de->bld", grad_qkv_b, b_qkv)
    shares = (
        lax.psum_scatter(g_w_qkv * factor, "shard", scatter_dimension=0, tiled=True),
        lax.psum_scatter(g_bias_q * factor, "shard", scatter_dimension=0, tiled=True),
        lax.psum_scatter(g_bias_v * factor, "shard", scatter_dimension=0, tiled=True),
        lax.psum_scatter(g_w_out * factor, "shard", scatter_dimension=0, tiled=True),
        lax.psum_scatter(g_bias_out * factor, "shard", scatter_dimension=0, tiled=True),
        lax.psum_scatter(g_gain_attn * factor, "shard", scatter_dimension=0, tiled=True),
        lax.psum_scatter(g_shift_attn * factor, "shard", scatter_dimension=0, tiled=True),
        lax.psum_scatter(g_w_in * factor, "shard", scatter_dimension=0, tiled=True),
        lax.psum_scatter(g_bias_in * factor, "shard", scatter_dimension=0, tiled=True),
        lax.psum_scatter(g_w_back * factor, "shard", scatter_dimension=0, tiled=True),
        lax.psum_scatter(g_bias_back * factor, "shard", scatter_dimension=0, tiled=True),
        lax.psum_scatter(g_gain_ffn * factor, "shard", scatter_dimension=0, tiled=True),
        lax.psum_scatter(g_shift_ffn * factor, "shard", scatter_dimension=0, tiled=True),
    )
    s_qkv, s_bq, s_bv, s_out, s_bo, s_ga, s_sa, s_in, s_bi, s_back, s_bb, s_gf, s_sf = shares
    summed = lax.psum(
        (s_qkv, s_bq, s_bv, s_out, s_bo, s_ga, s_sa, s_in, s_bi, s_back, s_bb, s_gf, s_sf),
        "replica",
    )
    r_qkv, r_bq, r_bv, r_out, r_bo, r_ga, r_sa, r_in, r_bi, r_back, r_bb, r_gf, r_sf = summed
    return (
        block_out.reshape(group * span, width),
        grad_input.reshape(group * span, width),
        r_qkv,
        r_bq,
        r_bv,
        r_out,
        r_bo,
        r_ga,
        r_sa,
        r_in,
        r_bi,
        r_back,
        r_bb,
        r_gf,
        r_sf,
    )


def solution(mesh):
    placed = (
        P(("replica", "shard"), None),
        P(("replica", "shard")),
        P(("replica", "shard"), None),
        P("shard", None),
        P("shard"),
        P("shard"),
        P("shard", None),
        P("shard"),
        P("shard"),
        P("shard"),
        P("shard", None),
        P("shard"),
        P("shard", None),
        P("shard"),
        P("shard"),
        P("shard"),
    )
    return jax.shard_map(
        on_device,
        mesh=mesh,
        in_specs=placed,
        out_specs=(
            P(("replica", "shard"), None),
            P(("replica", "shard"), None),
            P("shard", None),
            P("shard"),
            P("shard"),
            P("shard", None),
            P("shard"),
            P("shard"),
            P("shard"),
            P("shard", None),
            P("shard"),
            P("shard", None),
            P("shard"),
            P("shard"),
            P("shard"),
        ),
        check_vma=False,
    )
```

profile of v0, /device:TPU:0, one launch (start us, length us, event | category | flops | bytes accessed | tf_op | source)
XLA Modules:
  0.0 862.2 jit_solution(6676754043816239792)
XLA Ops:
  10.8 5.3 all-gather.1
  16.2 4.4 all-gather
  20.6 4.4 all-gather.2
  25.0 4.7 all-gather.3
  29.7 4.5 all-gather.4
  34.3 4.5 all-gather.6
  39.4 4.5 all-gather.7
  44.0 4.5 all-gather.8
  49.1 4.6 all-gather.5
  55.5 6.5 all-gather.14.cloned.1.call-done
  62.0 3.1 convolution_bitcast_fusion
  66.2 1.0 copy.55
  68.1 1.9 fusion.63
  71.1 1.4 fusion.34
  72.5 13.8 %all-gather.16.cloned.1.call-done = bf16[768,768]{1,0:T(8,128)(2,1)} async-done(((bf16[384,768]{1,0:T(8,128)(2,1)}), bf16[768,768]{1,0:T(8,128)(2,1)}) %all-gather.16.cloned.1.call-update) | async-done | bytes 1179664 | tf_op jit(solution)/shard_map/all_gather | solution.py:61
  86.3 2.0 fusion.64
  90.0 60.5 %all-gather.18.cloned.1.call-done = bf16[768,3072]{1,0:T(8,128)(2,1)} async-done(((bf16[384,3072]{1,0:T(8,128)(2,1)}), bf16[768,3072]{1,0:T(8,128)(2,1)}) %all-gather.18.cloned.1.call-update) | async-done | bytes 4718608 | tf_op jit(solution)/shard_map/all_gather | solution.py:65
  150.5 6.6 multiply_convert_fusion.1
  157.1 57.5 %all-gather.20.cloned.1.call-done = bf16[3072,768]{1,0:T(8,128)(2,1)} async-done(((bf16[1536,768]{1,0:T(8,128)(2,1)}), bf16[3072,768]{1,0:T(8,128)(2,1)}) %all-gather.20.cloned.1.call-update) | async-done | bytes 4718608 | tf_op jit(solution)/shard_map/all_gather | solution.py:67
  214.6 4.7 fusion.65
  219.5 1.0 multiply_reduce_fusion.1
  220.6 1.7 fusion.59
  222.3 3.0 fusion.68
  225.4 2.2 multiply_reduce_fusion.2
  229.4 1.9 convolution_multiply_fusion.3
  231.6 1.4 log_add_fusion
  232.9 2.8 convolution_convert_fusion
  235.7 1.9 copy.57
  237.6 3.5 fusion.69
  241.1 5.1 fusion.35
  246.2 5.7 fusion.62
  251.9 1.8 fusion.61
  254.4 4.0 multiply_bitcast_fusion
  258.5 1.0 copy-done.2
  260.1 5.2 convolution_multiply_fusion.1
  265.3 1.1 copy-done.7
  267.0 5.1 convolution_multiply_fusion
  272.2 81.9 %reduce-scatter.5.cloned.1.call-done = f32[384,2304]{0,1:T(8,128)} async-done(((f32[768,2304]{0,1:T(8,128)}), f32[384,2304]{0,1:T(8,128)}) %reduce-scatter.5.cloned.1.call-update) | async-done | bytes 3538960 | tf_op jit(solution)/shard_map/reduce_scatter | solution.py:165
  354.1 113.0 %reduce-scatter.9.cloned.1.call-done = f32[384,3072]{1,0:T(8,128)} async-done(((f32[768,3072]{1,0:T(8,128)}), f32[384,3072]{1,0:T(8,128)}) %reduce-scatter.9.cloned.1.call-update) | async-done | bytes 4718608 | tf_op jit(solution)/shard_map/reduce_scatter | solution.py:172
  467.1 113.0 %reduce-scatter.11.cloned.1.call-done = f32[1536,768]{1,0:T(8,128)} async-done(((f32[3072,768]{1,0:T(8,128)}), f32[1536,768]{1,0:T(8,128)}) %reduce-scatter.11.cloned.1.call-update) | async-done | bytes 4718608 | tf_op jit(solution)/shard_map/reduce_scatter | solution.py:174
  582.9 7.5 all-reduce.11
  591.0 62.7 %all-reduce.9 = (f32[384]{0:T(512)}, f32[384]{0:T(512)}, f32[384]{0:T(512)}, f32[384]{0:T(512)}, f32[384]{0:T(512)}, /*index=5*/f32[1536]{0:T(1024)}, f32[384]{0:T(512)}, f32[384]{0:T(512)}, f32[384]{0:T(512)}) all-reduce(f32[384]{0:T(512)S(1)} %dynamic-slice.1, ...), channel_id=1, replica_groups=mesh['replica'=16,'shard'=2] {'replica'}, use_global_device_ids=true, to_apply=%region_15.16 | all-reduce | flops 4608 | bytes 36864 | tf_op jit(solution)/shard_map/psum | solution.py:180
  653.8 4.1 convolution_add_fusion.2
  657.9 183.6 %all-reduce.14.cloned.1.call-done = (f32[384,2304]{0,1:T(8,128)}, f32[384,768]{1,0:T(8,128)}, f32[384,3072]{1,0:T(8,128)}, f32[1536,768]{1,0:T(8,128)}) async-done(((f32[384,2304]{0,1:T(8,128)}, f32[384,768]{1,0:T(8,128)}, f32[384,3072]{1,0:T(8,128)}, f32[1536,768]{1,0:T(8,128)}), (f32[384,2304]{0,1:T(8,128)}, f32[384,768]{1,0:T(8,128)}, f32[384,3072]{1,0:T(8,128)}, ...) | async-done | bytes 14155792 | tf_op jit(solution)/shard_map/psum | solution.py:180
  841.5 5.2 copy.61
  846.8 1.0 copy.71
  847.8 5.7 copy.72
  853.5 2.2 copy.73
  (191 shorter events, 17.1 us)
Async XLA Ops:
  7.2 3.6 copy-start.38
  7.2 8.9 %copy-start.39 = (bf16[384]{0:T(512)(128)(2,1)S(1)}, bf16[384]{0:T(512)(128)(2,1)}, u32[]{:S(2)}) copy-start(bf16[384]{0:T(512)(128)(2,1)} %param.21) | copy-start | bytes 2308
  7.2 13.3 %copy-start.40 = (bf16[384]{0:T(512)(128)(2,1)S(1)}, bf16[384]{0:T(512)(128)(2,1)}, u32[]{:S(2)}) copy-start(bf16[384]{0:T(512)(128)(2,1)} %param.23) | copy-start | bytes 2308
  7.2 17.8 %copy-start.41 = (bf16[384]{0:T(512)(128)(2,1)S(1)}, bf16[384]{0:T(512)(128)(2,1)}, u32[]{:S(2)}) copy-start(bf16[384]{0:T(512)(128)(2,1)} %param.24) | copy-start | bytes 2308
  7.2 22.5 %copy-start.42 = (bf16[384]{0:T(512)(128)(2,1)S(1)}, bf16[384]{0:T(512)(128)(2,1)}, u32[]{:S(2)}) copy-start(bf16[384]{0:T(512)(128)(2,1)} %param.25) | copy-start | bytes 2308
  7.2 54.8 %all-gather.14.cloned.1.call-start = ((), (), s32[]{:S(2)}) async-start(), calls=%async_computation.4 | async-start | bytes 5308416 | tf_op jit(solution)/shard_map/all_gather | solution.py:58
  8.0 26.3 %copy-start.43 = (bf16[384]{0:T(512)(128)(2,1)S(1)}, bf16[384]{0:T(512)(128)(2,1)}, u32[]{:S(2)}) copy-start(bf16[384]{0:T(512)(128)(2,1)} %param.29) | copy-start | bytes 2308
  8.0 31.4 %copy-start.44 = (bf16[384]{0:T(512)(128)(2,1)S(1)}, bf16[384]{0:T(512)(128)(2,1)}, u32[]{:S(2)}) copy-start(bf16[384]{0:T(512)(128)(2,1)} %param.30) | copy-start | bytes 2308
  8.0 36.0 %copy-start.45 = (bf16[384]{0:T(512)(128)(2,1)S(1)}, bf16[384]{0:T(512)(128)(2,1)}, u32[]{:S(2)}) copy-start(bf16[384]{0:T(512)(128)(2,1)} %param.31) | copy-start | bytes 2308
  8.0 41.1 %copy-start.34 = (bf16[1536]{0:T(1024)(128)(2,1)S(1)}, bf16[1536]{0:T(1024)(128)(2,1)}, u32[]{:S(2)}) copy-start(bf16[1536]{0:T(1024)(128)(2,1)} %param.27) | copy-start | bytes 9220
  8.0 54.0 %copy-start.5 = (bf16[256,768]{1,0:T(8,128)(2,1)S(1)}, bf16[256,768]{1,0:T(8,128)(2,1)}, u32[]{:S(2)}) copy-start(bf16[256,768]{1,0:T(8,128)(2,1)} %param.16) | copy-start | bytes 1179652
  8.0 78.3 %all-gather.16.cloned.1.call-start = ((), (), s32[]{:S(2)}) async-start(), calls=%async_computation.5 | async-start | bytes 1769472 | tf_op jit(solution)/shard_map/all_gather | solution.py:61
  8.8 141.8 %all-gather.18.cloned.1.call-start = ((), (), s32[]{:S(2)}) async-start(), calls=%async_computation.6 | async-start | bytes 7077888 | tf_op jit(solution)/shard_map/all_gather | solution.py:65
  9.5 205.1 %all-gather.20.cloned.1.call-start = ((), (), s32[]{:S(2)}) async-start(), calls=%async_computation.7 | async-start | bytes 7077888 | tf_op jit(solution)/shard_map/all_gather | solution.py:67
  10.1 262.1 %reduce-scatter.7.cloned.1.call-start = ((), (), s32[]{:S(2)}) async-start(), calls=%async_computation.9 | async-start | bytes 3538944 | tf_op jit(solution)/shard_map/reduce_scatter | solution.py:168
  68.1 3.0 copy-start.15
  88.3 139.3 %copy-start.23 = (f32[256]{0:T(256)}, f32[256]{0:T(256)S(1)}, u32[]{:S(2)}) copy-start(f32[256]{0:T(256)S(1)} %broadcast_multiply_fusion.14) | copy-start | bytes 3076
  214.6 7.7 slice-start.4
  214.6 4.9 copy-start.12
  214.6 4.9 copy-start.37
  214.6 6.0 copy-start.25
  214.6 7.7 slice-start.5
  219.3 3.0 copy-start.47
  220.6 4.8 slice-start.2
  222.3 3.1 copy-start.6
  222.3 3.0 copy-start.1
  222.3 3.0 copy-start.30
  222.3 3.0 slice-start.3
  225.4 4.0 copy-start.11
  231.3 122.8 %reduce-scatter.5.cloned.1.call-start = ((), (), s32[]{:S(2)}) async-start(), calls=%async_computation.8 | async-start | bytes 10616832 | tf_op jit(solution)/shard_map/reduce_scatter | solution.py:165
  258.4 208.6 %reduce-scatter.9.cloned.1.call-start = ((), (), s32[]{:S(2)}) async-start(), calls=%async_computation.10 | async-start | bytes 14155776 | tf_op jit(solution)/shard_map/reduce_scatter | solution.py:172
  265.3 314.8 %reduce-scatter.11.cloned.1.call-start = ((), (), s32[]{:S(2)}) async-start(), calls=%async_computation.11 | async-start | bytes 14155776 | tf_op jit(solution)/shard_map/reduce_scatter | solution.py:174
  272.1 569.4 %all-reduce.14.cloned.1.call-start = ((), (), s32[]{:S(2)}) async-start(), calls=%async_computation.12 | async-start | bytes 28311552 | tf_op jit(solution)/shard_map/psum | solution.py:180
  580.0 2.6 copy-start.33
  580.0 2.7 copy-start.36
  580.1 2.7 copy-start.26
  580.1 2.7 copy-start.27
  580.1 2.7 copy-start.35
  580.1 2.7 copy-start.28
  580.1 2.7 copy-start.29
  580.1 2.7 copy-start.32
  580.1 73.7 %copy-start.4 = (f32[256,768]{1,0:T(8,128)S(1)}, f32[256,768]{1,0:T(8,128)}, u32[]{:S(2)}) copy-start(f32[256,768]{1,0:T(8,128)} %copy-done.3) | copy-start | bytes 2359300
  580.1 73.7 %copy-start.10 = (bf16[1,256,12,64]{1,3,2,0:T(8,128)(2,1)S(1)}, bf16[1,256,12,64]{1,3,2,0:T(8,128)(2,1)}, u32[]{:S(2)}) copy-start(bf16[1,256,12,64]{1,3,2,0:T(8,128)(2,1)} %copy-done.9) | copy-start | bytes 1179652
  580.1 73.7 %copy-start.18 = (bf16[12,64,256]{2,1,0:T(8,128)(2,1)S(1)}, bf16[12,64,256]{2,1,0:T(8,128)(2,1)}, u32[]{:S(2)}) copy-start(bf16[12,64,256]{2,1,0:T(8,128)(2,1)} %fusion.35) | copy-start | bytes 1179652
  580.1 73.7 %copy-start.20 = (bf16[1,256,12,64]{1,3,2,0:T(8,128)(2,1)S(1)}, bf16[1,256,12,64]{1,3,2,0:T(8,128)(2,1)}, u32[]{:S(2)}) copy-start(bf16[1,256,12,64]{1,3,2,0:T(8,128)(2,1)} %get-tuple-element.100) | copy-start | bytes 1179652
  841.5 5.3 copy-start.16
  846.8 6.7 slice-start
  847.8 5.7 slice-start.1
  (15 other events, 20.7 us)
Sparse Core Ops, SparseCore 0:
  9.6 52.3 all-gather.13
  63.5 22.7 all-gather.15
  87.9 62.6 all-gather.17
  151.9 62.6 all-gather.19
  231.4 34.7 reduce-scatter.6
  268.4 85.6 reduce-scatter.4
  356.4 110.6 reduce-scatter.8
  469.4 110.6 reduce-scatter.10
  584.6 256.8 all-reduce.13
where the time goes:
time: 863 us; the launch traced here: 862 us
  waiting for transfers between devices  632 us (73%)
  blocking collectives  112 us (13%)
  matrix products  64 us (7%)
  local copies, waits for them, and re-layouts  28.7 us (3%)
  between operations  16.4 us (2%)
    psum x1, waiting for transfers between devices, on_device(): lax.psum((s_qkv, s_bq, s_bv, s_out, s_bo, s_ga, s_sa, s_in, s_bi, s_back,...  184 us
    reduce_scatter x1, waiting for transfers between devices, on_device(): lax.psum_scatter(g_w_back * factor, 'shard', scatter_dimension=0, tiled=T...  113 us
    reduce_scatter x1, waiting for transfers between devices, on_device(): lax.psum_scatter(g_w_in * factor, 'shard', scatter_dimension=0, tiled=True)  113 us
    reduce_scatter x1, waiting for transfers between devices, on_device(): lax.psum_scatter(g_w_qkv * factor, 'shard', scatter_dimension=0, tiled=True)  81.9 us
    dot_general x18, matrix products, product(): return jnp.einsum(form, left, right, preferred_element_type=jnp.float32)  64 us
    psum x1, blocking collectives, on_device(): lax.psum((s_qkv, s_bq, s_bv, s_out, s_bo, s_ga, s_sa, s_in, s_bi, s_back,...  62.7 us
    all_gather x1, waiting for transfers between devices, on_device(): lax.all_gather(w_in, 'shard', axis=0, tiled=True)  60.5 us
    all_gather x1, waiting for transfers between devices, on_device(): lax.all_gather(w_back, 'shard', axis=0, tiled=True)  57.5 us
  transfers between devices with their start and end apart: 9, of which 8 were waited for; matrix products, arithmetic and copies ran while one was open for 7% of the time, Pallas kernels for 0%

commit v1 on v0

--- a/solution.py
+++ b/solution.py
@@ -5,6 +5,15 @@
 
 HEADS = 12
 HEAD_DIM = 64
+
+
+def _name_slots(array_here):
+    return jnp.concatenate(
+        lax.all_to_all(
+            jnp.stack([array_here for _ in range(lax.axis_size("shard"))], axis=0), "shard", 0, 0
+        ),
+        axis=0,
+    )
 
 
 def product(form, left, right):
@@ -64,7 +73,7 @@
         lax.all_gather(shift_attn, "shard", axis=0, tiled=True),
         lax.all_gather(w_in, "shard", axis=0, tiled=True),
         lax.all_gather(bias_in, "shard", axis=0, tiled=True),
-        lax.all_gather(w_back, "shard", axis=0, tiled=True),
+        _name_slots(w_back),
         lax.all_gather(bias_back, "shard", axis=0, tiled=True),
         lax.all_gather(gain_ffn, "shard", axis=0, tiled=True),
         lax.all_gather(shift_ffn, "shard", axis=0, tiled=True),

time: 863 us -> 899 us (1.042)
  blocking collectives: 112 us -> 198 us
  waiting for transfers between devices: 632 us -> 567 us
    all_gather x1, blocking collectives: 4.51 us -> 92 us  [on_device(): lax.all_gather(bias_back, 'shard', axis=0, tiled=True)]
    all_gather x1, waiting for transfers between devices: 60.5 us -> 24 us  [on_device(): lax.all_gather(w_in, 'shard', axis=0, tiled=True)]
    all_gather x1, waiting for transfers between devices: 13.8 us -> 0.01 us  [on_device(): lax.all_gather(w_out, 'shard', axis=0, tiled=True)]
    unnamed x131 -> x123, local copies, waits for them, and re-layouts: 22.5 us -> 22.5 us
  transfers between devices with their start and end apart: 9 -> 10, of which waited for: 8 -> 6; matrix products, arithmetic and copies ran while one was open for 7% -> 8% of each run, Pallas kernels for 0% -> 0%
where the time goes in v1:
time: 899 us; the launch traced here: 898 us
  waiting for transfers between devices  567 us (63%)
  blocking collectives  198 us (22%)
  matrix products  71.1 us (8%)
  local copies, waits for them, and re-layouts  28.7 us (3%)
  between operations  16.4 us (2%)
  other arithmetic  11.3 us (1%)
    psum x1, waiting for transfers between devices, on_device(): lax.psum((s_qkv, s_bq, s_bv, s_out, s_bo, s_ga, s_sa, s_in, s_bi, s_back,...  184 us
    reduce_scatter x1, waiting for transfers between devices, on_device(): lax.psum_scatter(g_w_back * factor, 'shard', scatter_dimension=0, tiled=T...  113 us
    reduce_scatter x1, waiting for transfers between devices, on_device(): lax.psum_scatter(g_w_in * factor, 'shard', scatter_dimension=0, tiled=True)  113 us
    all_gather x1, blocking collectives, on_device(): lax.all_gather(bias_back, 'shard', axis=0, tiled=True)  92 us
    reduce_scatter x1, waiting for transfers between devices, on_device(): lax.psum_scatter(g_w_qkv * factor, 'shard', scatter_dimension=0, tiled=True)  81.9 us
    dot_general x18, matrix products, product(): return jnp.einsum(form, left, right, preferred_element_type=jnp.float32)  71.1 us
    psum x1, blocking collectives, on_device(): lax.psum((s_qkv, s_bq, s_bv, s_out, s_bo, s_ga, s_sa, s_in, s_bi, s_back,...  62.8 us
    all_gather x1, waiting for transfers between devices, on_device(): lax.all_gather(w_back, 'shard', axis=0, tiled=True)  48.6 us
  transfers between devices with their start and end apart: 10, of which 6 were waited for; matrix products, arithmetic and copies ran while one was open for 8% of the time, Pallas kernels for 0%

profile of v1, /device:TPU:0, one launch (start us, length us, event | category | flops | bytes accessed | tf_op | source)
XLA Modules:
  0.0 898.5 jit_solution(4671556166196013117)
XLA Ops:
  9.4 2.6 pad_maximum_fusion
  12.1 5.9 all-to-all-start
  18.6 92.0 %all-gather.6 = bf16[2,1,384]{2,1,0:T(2,128)(2,1)S(1)} all-gather(bf16[1,1,384]{2,1,0:T(2,128)(2,1)S(1)} %reshape.416), channel_id=1, replica_groups=mesh['replica'=16,'shard'=2] {'shard'}, dimensions={0}, use_global_device_ids=true | all-gather | bytes 2304 | tf_op jit(solution)/shard_map/all_gather | solution.py:77
  111.2 4.6 all-gather.5
  116.5 4.5 all-gather.2
  121.1 4.4 all-gather.1
  125.5 4.4 all-gather
  131.0 4.3 all-gather.4
  135.4 4.5 all-gather.3
  140.6 4.5 all-gather.7
  145.1 4.5 all-gather.8
  150.3 3.1 convolution_bitcast_fusion
  155.4 1.0 copy.55
  156.3 1.9 fusion.63
  159.3 1.4 fusion.34
  160.8 2.0 fusion.64
  164.5 24.0 %all-gather.18.cloned.1.call-done = bf16[768,3072]{1,0:T(8,128)(2,1)} async-done(((bf16[384,3072]{1,0:T(8,128)(2,1)}), bf16[768,3072]{1,0:T(8,128)(2,1)}) %all-gather.18.cloned.1.call-update) | async-done | bytes 4718608 | tf_op jit(solution)/shard_map/all_gather | solution.py:74
  188.5 6.6 multiply_convert_fusion.1
  195.0 5.6 fusion.65
  200.9 1.0 multiply_reduce_fusion.1
  201.9 2.0 fusion.59
  203.9 48.6 %all-gather.20.cloned.1.call-done = bf16[3072,768]{1,0:T(8,128)(2,1)} async-done(((bf16[1536,768]{1,0:T(8,128)(2,1)}), bf16[3072,768]{1,0:T(8,128)(2,1)}) %all-gather.20.cloned.1.call-update) | async-done | bytes 4718608 | tf_op jit(solution)/shard_map/all_gather | solution.py:130
  252.5 6.1 fusion.68
  258.6 5.2 multiply_reduce_fusion.2
  265.7 1.9 convolution_multiply_fusion.3
  267.8 1.3 log_add_fusion
  269.2 2.8 convolution_convert_fusion
  271.9 1.9 copy.57
  273.8 3.5 fusion.69
  277.4 5.1 fusion.35
  282.5 5.7 fusion.62
  288.2 1.8 fusion.61
  290.7 4.0 multiply_bitcast_fusion
  294.7 1.0 copy-done.2
  296.3 5.2 convolution_multiply_fusion.1
  301.6 1.1 copy-done.8
  303.2 5.1 convolution_multiply_fusion
  308.5 81.9 %reduce-scatter.5.cloned.1.call-done = f32[384,2304]{0,1:T(8,128)} async-done(((f32[768,2304]{0,1:T(8,128)}), f32[384,2304]{0,1:T(8,128)}) %reduce-scatter.5.cloned.1.call-update) | async-done | bytes 3538960 | tf_op jit(solution)/shard_map/reduce_scatter | solution.py:174
  390.4 113.0 %reduce-scatter.9.cloned.1.call-done = f32[384,3072]{1,0:T(8,128)} async-done(((f32[768,3072]{1,0:T(8,128)}), f32[384,3072]{1,0:T(8,128)}) %reduce-scatter.9.cloned.1.call-update) | async-done | bytes 4718608 | tf_op jit(solution)/shard_map/reduce_scatter | solution.py:181
  503.3 113.0 %reduce-scatter.11.cloned.1.call-done = f32[1536,768]{1,0:T(8,128)} async-done(((f32[3072,768]{1,0:T(8,128)}), f32[1536,768]{1,0:T(8,128)}) %reduce-scatter.11.cloned.1.call-update) | async-done | bytes 4718608 | tf_op jit(solution)/shard_map/reduce_scatter | solution.py:183
  619.1 7.5 all-reduce.11
  627.3 62.8 %all-reduce.9 = (f32[384]{0:T(512)}, f32[384]{0:T(512)}, f32[384]{0:T(512)}, f32[384]{0:T(512)}, f32[384]{0:T(512)}, /*index=5*/f32[1536]{0:T(1024)}, f32[384]{0:T(512)}, f32[384]{0:T(512)}, f32[384]{0:T(512)}) all-reduce(f32[384]{0:T(512)S(1)} %dynamic-slice.1, ...), channel_id=1, replica_groups=mesh['replica'=16,'shard'=2] {'replica'}, use_global_device_ids=true, to_apply=%region_15.16 | all-reduce | flops 4608 | bytes 36864 | tf_op jit(solution)/shard_map/psum | solution.py:189
  690.1 4.1 convolution_add_fusion.2
  694.2 183.5 %all-reduce.14.cloned.1.call-done = (f32[384,2304]{0,1:T(8,128)}, f32[384,768]{1,0:T(8,128)}, f32[384,3072]{1,0:T(8,128)}, f32[1536,768]{1,0:T(8,128)}) async-done(((f32[384,2304]{0,1:T(8,128)}, f32[384,768]{1,0:T(8,128)}, f32[384,3072]{1,0:T(8,128)}, f32[1536,768]{1,0:T(8,128)}), (f32[384,2304]{0,1:T(8,128)}, f32[384,768]{1,0:T(8,128)}, f32[384,3072]{1,0:T(8,128)}, ...) | async-done | bytes 14155792 | tf_op jit(solution)/shard_map/psum | solution.py:189
  877.8 5.2 copy.61
  883.0 1.0 copy.71
  884.0 5.7 copy.72
  889.8 2.2 copy.73
  (184 shorter events, 17.1 us)
Async XLA Ops:
  7.2 2.2 copy-start.3
  7.2 143.1 %all-gather.14.cloned.1.call-start = ((), (), s32[]{:S(2)}) async-start(), calls=%async_computation.5 | async-start | bytes 5308416 | tf_op jit(solution)/shard_map/all_gather | solution.py:67
  7.9 152.9 %all-gather.16.cloned.1.call-start = ((), (), s32[]{:S(2)}) async-start(), calls=%async_computation.6 | async-start | bytes 1769472 | tf_op jit(solution)/shard_map/all_gather | solution.py:70
  8.7 179.8 %all-gather.18.cloned.1.call-start = ((), (), s32[]{:S(2)}) async-start(), calls=%async_computation.7 | async-start | bytes 7077888 | tf_op jit(solution)/shard_map/all_gather | solution.py:74
  12.0 6.6 copy-start.39
  12.0 99.2 %copy-start.35 = (bf16[1536]{0:T(1024)(128)(2,1)S(1)}, bf16[1536]{0:T(1024)(128)(2,1)}, u32[]{:S(2)}) copy-start(bf16[1536]{0:T(1024)(128)(2,1)} %param.27) | copy-start | bytes 9220
  12.0 104.5 %copy-start.40 = (bf16[384]{0:T(512)(128)(2,1)S(1)}, bf16[384]{0:T(512)(128)(2,1)}, u32[]{:S(2)}) copy-start(bf16[384]{0:T(512)(128)(2,1)} %param.23) | copy-start | bytes 2308
  12.0 109.0 %copy-start.41 = (bf16[384]{0:T(512)(128)(2,1)S(1)}, bf16[384]{0:T(512)(128)(2,1)}, u32[]{:S(2)}) copy-start(bf16[384]{0:T(512)(128)(2,1)} %param.20) | copy-start | bytes 2308
  12.0 113.4 %copy-start.42 = (bf16[384]{0:T(512)(128)(2,1)S(1)}, bf16[384]{0:T(512)(128)(2,1)}, u32[]{:S(2)}) copy-start(bf16[384]{0:T(512)(128)(2,1)} %param.21) | copy-start | bytes 2308
  12.0 119.0 %copy-start.43 = (bf16[384]{0:T(512)(128)(2,1)S(1)}, bf16[384]{0:T(512)(128)(2,1)}, u32[]{:S(2)}) copy-start(bf16[384]{0:T(512)(128)(2,1)} %param.25) | copy-start | bytes 2308
  12.0 123.4 %copy-start.44 = (bf16[384]{0:T(512)(128)(2,1)S(1)}, bf16[384]{0:T(512)(128)(2,1)}, u32[]{:S(2)}) copy-start(bf16[384]{0:T(512)(128)(2,1)} %param.24) | copy-start | bytes 2308
  12.1 128.5 %copy-start.45 = (bf16[384]{0:T(512)(128)(2,1)S(1)}, bf16[384]{0:T(512)(128)(2,1)}, u32[]{:S(2)}) copy-start(bf16[384]{0:T(512)(128)(2,1)} %param.30) | copy-start | bytes 2308
  12.1 133.0 %copy-start.46 = (bf16[384]{0:T(512)(128)(2,1)S(1)}, bf16[384]{0:T(512)(128)(2,1)}, u32[]{:S(2)}) copy-start(bf16[384]{0:T(512)(128)(2,1)} %param.31) | copy-start | bytes 2308
  12.1 138.2 %copy-start.6 = (bf16[256,768]{1,0:T(8,128)(2,1)S(1)}, bf16[256,768]{1,0:T(8,128)(2,1)}, u32[]{:S(2)}) copy-start(bf16[256,768]{1,0:T(8,128)(2,1)} %param.16) | copy-start | bytes 1179652
  12.1 182.9 %all-to-all-start = ((bf16[2,1536,768]{2,1,0:T(8,128)(2,1)}), bf16[2,1536,768]{2,1,0:T(8,128)(2,1)}, u32[]{:S(2)}, u32[]{:S(2)}) async-start(bf16[2,1536,768]{2,1,0:T(8,128)(2,1)} %pad_maximum_fusion), calls=%async_computation | async-start | bytes 9437184 | tf_op jit(solution)/shard_map/all_to_all | solution.py:12
  18.0 234.5 %all-gather.20.cloned.1.call-start = ((), (), s32[]{:S(2)}) async-start(), calls=%async_computation.8 | async-start | bytes 7077888 | tf_op jit(solution)/shard_map/all_gather | solution.py:130
  18.6 289.9 %reduce-scatter.7.cloned.1.call-start = ((), (), s32[]{:S(2)}) async-start(), calls=%async_computation.10 | async-start | bytes 3538944 | tf_op jit(solution)/shard_map/reduce_scatter | solution.py:177
  156.3 3.0 copy-start.16
  162.8 101.1 %copy-start.24 = (f32[256]{0:T(256)}, f32[256]{0:T(256)S(1)}, u32[]{:S(2)}) copy-start(f32[256]{0:T(256)S(1)} %broadcast_multiply_fusion.14) | copy-start | bytes 3076
  195.0 5.9 copy-start.13
  195.0 5.9 copy-start.38
  195.0 6.9 copy-start.26
  252.5 6.1 copy-start.1
  252.5 6.1 copy-start.7
  252.5 6.1 copy-start.31
  258.6 5.3 copy-start.14
  258.6 7.0 copy-start.12
  267.6 122.8 %reduce-scatter.5.cloned.1.call-start = ((), (), s32[]{:S(2)}) async-start(), calls=%async_computation.9 | async-start | bytes 10616832 | tf_op jit(solution)/shard_map/reduce_scatter | solution.py:174
  288.2 2.5 copy-start.18
  288.2 2.5 copy-start.20
  294.7 208.6 %reduce-scatter.9.cloned.1.call-start = ((), (), s32[]{:S(2)}) async-start(), calls=%async_computation.11 | async-start | bytes 14155776 | tf_op jit(solution)/shard_map/reduce_scatter | solution.py:181
  301.5 314.8 %reduce-scatter.11.cloned.1.call-start = ((), (), s32[]{:S(2)}) async-start(), calls=%async_computation.12 | async-start | bytes 14155776 | tf_op jit(solution)/shard_map/reduce_scatter | solution.py:183
  308.4 569.4 %all-reduce.14.cloned.1.call-start = ((), (), s32[]{:S(2)}) async-start(), calls=%async_computation.13 | async-start | bytes 28311552 | tf_op jit(solution)/shard_map/psum | solution.py:189
  616.3 2.5 copy-start.34
  616.3 2.7 copy-start.28
  616.3 2.7 copy-start.37
  616.3 2.7 copy-start.36
  616.3 2.7 copy-start.27
  616.3 2.7 copy-start.29
  616.3 2.7 copy-start.30
  616.3 2.8 copy-start.33
  616.4 73.7 %copy-start.5 = (f32[256,768]{1,0:T(8,128)S(1)}, f32[256,768]{1,0:T(8,128)}, u32[]{:S(2)}) copy-start(f32[256,768]{1,0:T(8,128)} %copy-done.4) | copy-start | bytes 2359300
  616.4 73.7 %copy-start.11 = (bf16[1,256,12,64]{1,3,2,0:T(8,128)(2,1)S(1)}, bf16[1,256,12,64]{1,3,2,0:T(8,128)(2,1)}, u32[]{:S(2)}) copy-start(bf16[1,256,12,64]{1,3,2,0:T(8,128)(2,1)} %copy-done.10) | copy-start | bytes 1179652
  616.4 73.7 %copy-start.19 = (bf16[12,64,256]{2,1,0:T(8,128)(2,1)S(1)}, bf16[12,64,256]{2,1,0:T(8,128)(2,1)}, u32[]{:S(2)}) copy-start(bf16[12,64,256]{2,1,0:T(8,128)(2,1)} %fusion.35) | copy-start | bytes 1179652
  616.4 73.7 %copy-start.21 = (bf16[1,256,12,64]{1,3,2,0:T(8,128)(2,1)S(1)}, bf16[1,256,12,64]{1,3,2,0:T(8,128)(2,1)}, u32[]{:S(2)}) copy-start(bf16[1,256,12,64]{1,3,2,0:T(8,128)(2,1)} %get-tuple-element.100) | copy-start | bytes 1179652
  877.8 5.3 copy-start.17
  883.0 6.7 slice-start
  884.0 5.7 slice-start.1
  (12 other events, 13.4 us)
Sparse Core Ops, SparseCore 0:
  9.5 90.0 all-gather.13
  101.2 22.9 all-gather.15
  125.7 62.6 all-gather.17
  189.8 62.6 all-gather.19
  267.7 34.7 reduce-scatter.6
  304.7 85.6 reduce-scatter.4
  392.7 110.6 reduce-scatter.8
  505.6 110.6 reduce-scatter.10
  620.9 256.8 all-reduce.13
